TPU v7x, 32 devices: a whole 2x2x4 slice. The times are simulated.
32 devices in a mesh: dp: 4 (over y, x), tensor: 8 (over z, core).
Axes of the slice: x: 2, y: 2, z: 4, core: 2. Of those that a mesh axis runs over, the one named last changes fastest.
Arguments:
- tokens: bfloat16 [8, 256, 8192], P('dp'), may hold values from -6 to 6
- segments: int32 [8, 256], P('dp'), may hold values from 0 to 3, never falling along the last dimension, each value on 1 to 128 neighbouring positions
- norm_gain: float32 [8192], replicated, may hold values from 0.25 to 3.5
- q_weight: bfloat16 [8192, 4096], P('dp', 'tensor'), may hold values from -1.3479223 to 1.3479223
- kv_weight: bfloat16 [2, 8192, 512], P(None, 'dp'), may hold values from -0.055242717 to 0.055242717
- o_weight: bfloat16 [4096, 8192], P('tensor', 'dp'), may hold values from -0.09375 to 0.09375
- basis_query: bfloat16 [8, 8192, 4096], P(None, 'dp', 'tensor'), may hold values from -11 to 11
- basis_output: bfloat16 [8, 4096, 8192], P(None, 'tensor', 'dp'), may hold values from -11 to 11
Outputs:
- next_query: bfloat16 [8192, 4096], P('dp', 'tensor')
- next_output: bfloat16 [4096, 8192], P('tensor', 'dp')
- coefficients: float32 [9], replicated
Inputs may be any that keep to these rules, and one draw needn't show every extreme that they name: `segments`: segment numbers never fall along a sequence.
All inputs are finite; a program needn't handle non-finite values.
Results may differ from a plain program's by a relative error of at most 0.018.
Values may be sent and summed in bfloat16 or wider, within the bound.
No kernel may reach another device: no remote copies, remote signals or barrier semaphores. Data moves between devices by JAX's collectives and lax.ppermute only.
A program may use at most 192 MiB of HBM per device.

v0:
```python
import math
import jax
import jax.numpy as jnp
from jax import lax
from jax.sharding import PartitionSpec as P

D = 8192
HD = 128
QH = 32
KVH = 4
K = 8
PRECISE = lax.Precision.HIGHEST
ROPE_BASE = 500000.0
NORM_EPS = 1e-05
BETA_EPS = 1e-06


def rope_tables(length, head_width):
    half_width = head_width // 2
    frequency = jnp.exp(
        jnp.arange(half_width, dtype=jnp.float32) * (-2.0 * math.log(ROPE_BASE) / head_width)
    )
    angles = jnp.arange(length, dtype=jnp.float32)[:, None] * frequency[None, :]
    return (jnp.cos(angles), jnp.sin(angles))


def rotate(vectors, cosine_table, sine_table):
    half_width = vectors.shape[-1] // 2
    front_half = vectors[..., :half_width]
    back_half = vectors[..., half_width:]
    return jnp.concatenate(
        [
            front_half * cosine_table - back_half * sine_table,
            front_half * sine_table + back_half * cosine_table,
        ],
        axis=-1,
    )


def attend(query, key_states, values, allowed):
    length = query.shape[1]
    head_width = query.shape[-1]
    cosine_table, sine_table = rope_tables(length, head_width)
    query = rotate(query, cosine_table[:, None, :], sine_table[:, None, :])
    key_states = rotate(key_states, cosine_table, sine_table)
    scores = jnp.einsum("slgd,smd->sglm", query, key_states, precision=PRECISE) * head_width ** (
        -0.5
    )
    scores = jnp.where(allowed[:, None, :, :], scores, -1e30)
    row_max = lax.stop_gradient(jnp.max(scores, axis=-1, keepdims=True))
    weights = jnp.exp(scores - row_max)
    probabilities = weights / jnp.sum(weights, axis=-1, keepdims=True)
    return jnp.einsum("sglm,smd->slgd", probabilities, values, precision=PRECISE)


def allowed_pairs(segments):
    length = segments.shape[1]
    position = jnp.arange(length, dtype=jnp.int32)
    causal = position[:, None] >= position[None, :]
    return jnp.logical_and(segments[:, :, None] == segments[:, None, :], causal[None])


def rms_normed(tokens, norm_gain):
    flat_rows = tokens.reshape(-1, tokens.shape[-1]).astype(jnp.float32)
    inv_rms = lax.rsqrt(jnp.mean(flat_rows * flat_rows, axis=1, keepdims=True) + NORM_EPS)
    return (flat_rows * inv_rms * norm_gain[None, :]).astype(jnp.bfloat16)


def block_products(left_rows, right_rows, block_count, factor):
    left_blocks = left_rows.reshape(block_count, -1, left_rows.shape[1])
    right_blocks = right_rows.reshape(block_count, -1, right_rows.shape[1])
    terms = (
        jnp.einsum("nta,ntb->nab", left_blocks, right_blocks, preferred_element_type=jnp.float32)
        * factor
    )
    rounded = lax.optimization_barrier(terms.astype(jnp.bfloat16))
    return jnp.sum(rounded.astype(jnp.float32), axis=0)


def body(tokens, segments, norm_gain, q_weight, kv_weight, o_weight, basis_query, basis_output):
    groups = lax.axis_size("dp")
    seq_count, length, model_width = tokens.shape
    row_count = seq_count * length
    col_count = q_weight.shape[1]
    heads_dev = col_count // HD
    group_size = QH // KVH
    qwidth = QH * HD
    query_scale = D ** (-0.5)
    output_scale = qwidth ** (-0.5)
    gn_scale = qwidth / (row_count * groups)
    param_count = 2.0 * D * qwidth
    normed = rms_normed(tokens, norm_gain)
    dir_query = basis_query[K - 1]
    dir_output = basis_output[K - 1]
    kv_head = lax.axis_index("tensor") * heads_dev // group_size
    kv_columns = lax.dynamic_slice_in_dim(kv_weight, kv_head * HD, HD, 2)
    kv_pair = jnp.concatenate([kv_columns[0], kv_columns[1]], axis=1)
    sum_query = jnp.dot(
        normed,
        lax.all_gather(q_weight, "dp", axis=0, tiled=True),
        preferred_element_type=jnp.float32,
    )
    sum_tangent = jnp.dot(
        normed,
        lax.all_gather(dir_query, "dp", axis=0, tiled=True),
        preferred_element_type=jnp.float32,
    )
    sum_pair = jnp.dot(
        normed,
        lax.all_gather(kv_pair, "dp", axis=0, tiled=True),
        preferred_element_type=jnp.float32,
    )
    query = sum_query.astype(jnp.bfloat16)
    tangent = (sum_tangent * query_scale).astype(jnp.bfloat16)
    key_states = sum_pair[:, :HD].astype(jnp.bfloat16)
    values = sum_pair[:, HD:].astype(jnp.bfloat16)
    allowed = allowed_pairs(segments)
    query_wide = query.astype(jnp.float32).reshape(seq_count, length, heads_dev, HD)
    tangent_wide = tangent.astype(jnp.float32).reshape(seq_count, length, heads_dev, HD)
    key_wide = key_states.astype(jnp.float32).reshape(seq_count, length, HD)
    value_wide = values.astype(jnp.float32).reshape(seq_count, length, HD)

    def attend_here(moving):
        return attend(moving, key_wide, value_wide, allowed)

    heads_out, tangent_heads = jax.jvp(attend_here, (query_wide,), (tangent_wide,))
    heads_out = heads_out.reshape(row_count, col_count).astype(jnp.bfloat16)
    tangent_heads = tangent_heads.reshape(row_count, col_count).astype(jnp.bfloat16)
    all_heads, all_tangent = (
        lax.all_gather(heads_out, "dp", axis=0, tiled=True),
        lax.all_gather(tangent_heads, "dp", axis=0, tiled=True),
    )
    group_term = jnp.dot(
        all_heads, dir_output, preferred_element_type=jnp.float32
    ) * output_scale + jnp.dot(all_tangent, o_weight, preferred_element_type=jnp.float32)
    tangent_columns = lax.psum(group_term.astype(jnp.bfloat16), "tensor")
    cot_heads = lax.psum_scatter(
        lax.dot_general(
            tangent_columns, o_weight, (((1,), (1,)), ((), ())), preferred_element_type=jnp.float32
        ).astype(jnp.bfloat16),
        "dp",
        scatter_dimension=0,
        tiled=True,
    ).astype(jnp.float32)
    gn_output = block_products(all_heads, tangent_columns, groups, gn_scale * output_scale)
    _, pullback = jax.vjp(attend_here, query_wide)
    cot_query = pullback(cot_heads.reshape(seq_count, length, heads_dev, HD))[0]
    cot_query = cot_query.reshape(row_count, col_count).astype(jnp.bfloat16)
    gn_query = lax.psum_scatter(
        (
            lax.dot_general(
                normed, cot_query, (((0,), (0,)), ((), ())), preferred_element_type=jnp.float32
            )
            * (gn_scale * query_scale)
        ).astype(jnp.bfloat16),
        "dp",
        scatter_dimension=0,
        tiled=True,
    ).astype(jnp.float32)

    def local_products(vec_query, vec_output):
        return jnp.sum(basis_query.astype(jnp.float32) * vec_query[None], axis=(1, 2)) + jnp.sum(
            basis_output.astype(jnp.float32) * vec_output[None], axis=(1, 2)
        )

    def remove(vec_query, vec_output, weights_now):
        return (
            vec_query
            - jnp.sum(weights_now[:, None, None] * basis_query.astype(jnp.float32), axis=0),
            vec_output
            - jnp.sum(weights_now[:, None, None] * basis_output.astype(jnp.float32), axis=0),
        )

    first_coeffs = lax.psum(local_products(gn_query, gn_output), ("dp", "tensor")) / param_count
    kept_query, kept_output = remove(gn_query, gn_output, first_coeffs)
    second_coeffs = (
        lax.psum(local_products(kept_query, kept_output), ("dp", "tensor")) / param_count
    )
    clean_query, clean_output = remove(kept_query, kept_output, second_coeffs)
    local_squares = jnp.sum(clean_query * clean_query) + jnp.sum(clean_output * clean_output)
    squares = lax.psum(local_squares, ("dp", "tensor")) / param_count
    beta = jnp.sqrt(squares + BETA_EPS)
    coefficients = jnp.concatenate([first_coeffs + second_coeffs, beta[None]])
    return (
        (clean_query / beta).astype(jnp.bfloat16),
        (clean_output / beta).astype(jnp.bfloat16),
        coefficients,
    )


def solution(mesh):
    return jax.shard_map(
        body,
        mesh=mesh,
        in_specs=(
            P("dp", None, None),
            P("dp", None),
            P(),
            P("dp", "tensor"),
            P(None, "dp", None),
            P("tensor", "dp"),
            P(None, "dp", "tensor"),
            P(None, "tensor", "dp"),
        ),
        out_specs=(P("dp", "tensor"), P("tensor", "dp"), P()),
        check_vma=False,
    )
```

profile of v0, /device:TPU:0, one launch (start us, length us, event | category | flops | bytes accessed | tf_op | source)
XLA Modules:
  0.0 907.9 jit_solution(18411011487311448735)
XLA Ops:
  7.2 1.4 dynamic-slice_bitcast_fusion.1
  8.7 1.1 pad_maximum_fusion
  9.8 3.0 slice.51
  13.0 0.7 all-gather.9.cloned.1.call-update
  13.7 5.1 multiply_reduce_fusion
  20.0 1.0 compare_and_fusion.1
  21.0 10.2 %fusion.9 = bf16[512,8192]{1,0:T(8,128)(2,1)} fusion(f32[8192]{0:T(1024)S(1)} %copy-done.18, f32[512]{0:T(512)S(1)} %bitcast.158, bf16[2,256,8192]{2,1,0:T(8,128)(2,1)} %param.8), kind=kLoop, calls=%fused_computation.18 | loop fusion | flops 16777216 | bytes 16812032 | tf_op jit(solution)/shard_map/convert_element_type | solution.py:66
  31.2 34.5 %all-gather.7.cloned.1.call-done = bf16[8192,256]{1,0:T(8,128)(2,1)} async-done(((bf16[2048,256]{1,0:T(8,128)(2,1)}), bf16[8192,256]{1,0:T(8,128)(2,1)}) %all-gather.7.cloned.1.call-update) | async-done | bytes 4194320 | tf_op jit(solution)/shard_map/all_gather | solution.py:110
  65.7 6.9 convolution_convert_fusion.2
  72.6 0.7 fusion.94
  73.3 0.8 multiply_subtract_fusion.2
  74.2 81.5 %all-gather.15.cloned.1.call-done = bf16[1,8192,512]{2,1,0:T(8,128)(2,1)} async-done(((bf16[1,2048,512]{2,1,0:T(8,128)(2,1)}), bf16[1,8192,512]{2,1,0:T(8,128)(2,1)}) %all-gather.15.cloned.1.call-update) | async-done | bytes 8388624 | tf_op jit(solution)/shard_map/all_gather | solution.py:105
  155.7 11.2 %fusion.44 = f32[512,512]{1,0:T(8,128)} fusion(bf16[512,8192]{1,0:T(8,128)(2,1)} %fusion.9, bf16[1,8192,512]{2,1,0:T(8,128)(2,1)} %all-gather.15.cloned.1.call-done), kind=kOutput, calls=%fused_computation.59 | convolution fusion | flops 4295753728 | bytes 17825792 | tf_op jit(solution)/shard_map/dot_general | solution.py:103
  166.9 1.7 reshape.217
  168.5 76.5 %all-gather.9.cloned.1.call-done = bf16[8192,512]{1,0:T(8,128)(2,1)} async-done(((bf16[2048,512]{1,0:T(8,128)(2,1)}), bf16[8192,512]{1,0:T(8,128)(2,1)}) %all-gather.9.cloned.1.call-update) | async-done | bytes 8388624 | tf_op jit(solution)/shard_map/all_gather | solution.py:100
  245.0 11.4 %fusion.47 = f32[512,512]{1,0:T(8,128)} fusion(bf16[512,8192]{1,0:T(8,128)(2,1)} %fusion.9, bf16[8192,512]{1,0:T(8,128)(2,1)} %all-gather.9.cloned.1.call-done), kind=kOutput, calls=%fused_computation.61 | convolution fusion | flops 4295491584 | bytes 17825792 | tf_op jit(solution)/shard_map/dot_general | solution.py:98
  256.5 2.5 reshape.215
  259.0 2.8 fusion.92
  261.8 0.6 multiply_subtract_fusion.1
  262.8 2.2 fusion.28
  265.0 2.7 fusion.30
  268.3 2.6 fusion.48
  270.9 1.3 copy.32
  272.3 0.9 copy.76
  273.6 3.8 fusion.51
  277.4 1.3 copy.27
  278.7 0.9 copy.77
  279.6 28.8 %all-gather.13.cloned.1.call-done = bf16[2048,512]{1,0:T(8,128)(2,1)} async-done(((bf16[512,512]{1,0:T(8,128)(2,1)}), bf16[2048,512]{1,0:T(8,128)(2,1)}) %all-gather.13.cloned.1.call-update) | async-done | bytes 2097168 | tf_op jit(solution)/shard_map/all_gather | solution.py:131
  308.5 9.9 %fusion.95 = f32[2048,2048]{1,0:T(8,128)} fusion(bf16[2048,512]{1,0:T(8,128)(2,1)} %all-gather.13.cloned.1.call-done, bf16[512,2048]{1,0:T(8,128)(2,1)S(1)} %copy-done), kind=kOutput, calls=%fused_computation.134 | convolution fusion | flops 4294967296 | bytes 20971520 | tf_op jit(solution)/shard_map/dot_general | solution.py:135
  318.4 27.0 %all-gather.11.cloned.1.call-done = bf16[2048,512]{1,0:T(8,128)(2,1)} async-done(((bf16[512,512]{1,0:T(8,128)(2,1)}), bf16[2048,512]{1,0:T(8,128)(2,1)}) %all-gather.11.cloned.1.call-update) | async-done | bytes 2097168 | tf_op jit(solution)/shard_map/all_gather | solution.py:130
  345.4 14.8 %add_convert_fusion = bf16[2048,2048]{1,0:T(8,128)(2,1)} fusion(f32[2048,2048]{1,0:T(8,128)} %fusion.95, bf16[2048,512]{1,0:T(8,128)(2,1)} %all-gather.11.cloned.1.call-done, bf16[8,512,2048]{2,1,0:T(8,128)(2,1)} %param.15), kind=kOutput, calls=%fused_computation.22 | convolution fusion | flops 4307550208 | bytes 29360128 | tf_op jit(solution)/shard_map/dot_general | solution.py:133
  360.3 175.6 %all-reduce.4.cloned.1.call-done = bf16[2048,2048]{1,0:T(8,128)(2,1)} async-done(((bf16[2048,2048]{1,0:T(8,128)(2,1)}), bf16[2048,2048]{1,0:T(8,128)(2,1)}) %all-reduce.4.cloned.1.call-update) | async-done | bytes 8388624 | tf_op jit(solution)/shard_map/psum | solution.py:136
  535.9 9.1 %convolution_convert_fusion = bf16[2048,512]{1,0:T(8,128)(2,1)} fusion(bf16[2048,2048]{1,0:T(8,128)(2,1)} %all-reduce.4.cloned.1.call-done, bf16[512,2048]{1,0:T(8,128)(2,1)S(1)} %copy-done), kind=kOutput, calls=%fused_computation.31 | convolution fusion | flops 4296015872 | bytes 12582912 | tf_op jit(solution)/shard_map/dot_general | solution.py:138
  545.3 0.9 copy.22
  546.2 10.0 %multiply_convert_fusion.2 = bf16[2,256,8192]{2,1,0:T(8,128)(2,1)} fusion(f32[8192]{0:T(1024)S(1)} %copy-done.19, f32[2,256]{1,0:T(2,128)S(1)} %copy-done.23, bf16[2,256,8192]{2,1,0:T(8,128)(2,1)} %param.8), kind=kLoop, calls=%fused_computation.23 | loop fusion | flops 16777216 | bytes 16812032 | tf_op jit(solution)/shard_map/convert_element_type | solution.py:66
  556.2 24.3 %reduce-scatter.3.cloned.1.call-done = bf16[512,512]{1,0:T(8,128)(2,1)} async-done(((bf16[2048,512]{1,0:T(8,128)(2,1)}), bf16[512,512]{1,0:T(8,128)(2,1)}) %reduce-scatter.3.cloned.1.call-update) | async-done | bytes 524304 | tf_op jit(solution)/shard_map/reduce_scatter | solution.py:137
  580.5 2.0 reshape.208
  582.5 1.3 copy.33
  583.8 1.6 multiply_reduce_fusion.3
  585.4 4.0 fusion.26
  590.7 7.1 multiply_convert_fusion.1
  597.8 1.6 copy-done.24
  599.4 10.3 %multiply_convert_fusion = bf16[4,512,2048]{2,1,0:T(8,128)(2,1)} fusion(bf16[4,512,512]{2,1,0:T(8,128)(2,1)S(1)} %bitcast.160, bf16[4,512,2048]{2,1,0:T(8,128)(2,1)} %bitcast.159), kind=kOutput, calls=%fused_computation.20 | convolution fusion | flops 4303355904 | bytes 18874368 | tf_op jit(solution)/shard_map/nta,ntb->nab/dot_general | solution.py:73
  609.7 5.9 convert_reduce_fusion
  615.6 2.0 copy-done.2
  617.6 7.8 fusion.4
  625.4 58.9 %reduce-scatter.5.cloned.1.call-done = bf16[2048,512]{1,0:T(8,128)(2,1)} async-done(((bf16[8192,512]{1,0:T(8,128)(2,1)}), bf16[2048,512]{1,0:T(8,128)(2,1)}) %reduce-scatter.5.cloned.1.call-update) | async-done | bytes 2097168 | tf_op jit(solution)/shard_map/reduce_scatter | solution.py:149
  684.3 2.2 convert_element_type.110
  686.5 8.0 fusion
  694.5 39.5 %psum.29 = f32[8]{0:T(128)S(1)} all-reduce(f32[8]{0:T(128)S(1)} %add.69), channel_id=1, replica_groups=mesh['dp'=4,'tensor'=8] {'dp','tensor'}, use_global_device_ids=true, to_apply=%region_11.12 | all-reduce | flops 8 | bytes 64 | tf_op jit(solution)/shard_map/psum | solution.py:174
  734.0 11.9 %fusion.5 = f32[512,2048]{1,0:T(8,128)S(1)} fusion(bf16[8,512,2048]{2,1,0:T(8,128)(2,1)} %param.15, f32[8]{0:T(128)S(1)} %broadcast_multiply_fusion.1), kind=kLoop, calls=%fused_computation.13 | loop fusion | flops 24117248 | bytes 20971552 | tf_op jit(solution)/shard_map/reduce_sum | solution.py:171
  746.0 14.8 %fusion.1 = f32[2048,512]{1,0:T(8,128)} fusion(bf16[8,2048,512]{2,1,0:T(8,128)(2,1)} %param.14, f32[8]{0:T(128)S(1)} %broadcast_multiply_fusion.1), kind=kLoop, calls=%fused_computation.9 | loop fusion | flops 24117248 | bytes 20971552 | tf_op jit(solution)/shard_map/reduce_sum | solution.py:169
  760.8 2.8 sub.60
  764.2 7.6 fusion.6
  771.7 3.1 convert_subtract_fusion
  775.2 5.4 fusion.2
  780.6 40.9 %psum.30 = f32[8]{0:T(128)S(1)} all-reduce(f32[8]{0:T(128)S(1)} %add.70), channel_id=1, replica_groups=mesh['dp'=4,'tensor'=8] {'dp','tensor'}, use_global_device_ids=true, to_apply=%region_16.17 | all-reduce | flops 8 | bytes 64 | tf_op jit(solution)/shard_map/psum | solution.py:177
  821.5 11.9 %fusion.7 = f32[512,2048]{1,0:T(8,128)S(1)} fusion(bf16[8,512,2048]{2,1,0:T(8,128)(2,1)} %param.15, f32[8]{0:T(128)S(1)} %get-tuple-element.32), kind=kLoop, calls=%fused_computation.15 | loop fusion | flops 24117248 | bytes 20971552 | tf_op jit(solution)/shard_map/reduce_sum | solution.py:171
  833.5 12.1 %fusion.3 = f32[2048,512]{1,0:T(8,128)S(1)} fusion(bf16[8,2048,512]{2,1,0:T(8,128)(2,1)} %param.14, f32[8]{0:T(128)S(1)} %get-tuple-element.32), kind=kLoop, calls=%fused_computation.11 | loop fusion | flops 24117248 | bytes 20971552 | tf_op jit(solution)/shard_map/reduce_sum | solution.py:169
  845.6 3.7 multiply_reduce_fusion.1
  849.2 3.7 multiply_reduce_fusion.2
  854.2 39.1 %psum.31 = f32[]{:T(128)} all-reduce(f32[]{:T(128)S(6)} %add.71), channel_id=1, replica_groups=mesh['dp'=4,'tensor'=8] {'dp','tensor'}, use_global_device_ids=true, to_apply=%region_21.22 | all-reduce | flops 1 | bytes 8 | tf_op jit(solution)/shard_map/psum | solution.py:181
  894.0 4.1 divide_convert_fusion
  898.2 1.9 divide_convert_fusion.1
  (103 shorter events, 6.0 us)
Async XLA Ops:
  7.2 301.3 %copy-start = (bf16[512,2048]{1,0:T(8,128)(2,1)S(1)}, bf16[512,2048]{1,0:T(8,128)(2,1)}, u32[]{:S(2)}) copy-start(bf16[512,2048]{1,0:T(8,128)(2,1)} %param.13) | copy-start | bytes 6291460
  7.2 58.6 %all-gather.7.cloned.1.call-start = ((), (), s32[]{:S(2)}) async-start(), calls=%async_computation.2 | async-start | bytes 5242880 | tf_op jit(solution)/shard_map/all_gather | solution.py:110
  9.8 145.9 %all-gather.15.cloned.1.call-start = ((), (), s32[]{:S(2)}) async-start(), calls=%async_computation.9 | async-start | bytes 10485760 | tf_op jit(solution)/shard_map/all_gather | solution.py:105
  12.9 232.1 %all-gather.9.cloned.1.call-start = ((), (), s32[]{:S(2)}) async-start(), calls=%async_computation.3 | async-start | bytes 10485760 | tf_op jit(solution)/shard_map/all_gather | solution.py:100
  13.6 6.3 copy-start.22
  13.7 7.3 copy-start.18
  13.7 294.8 %all-gather.13.cloned.1.call-start = ((), (), s32[]{:S(2)}) async-start(), calls=%async_computation.5 | async-start | bytes 2621440 | tf_op jit(solution)/shard_map/all_gather | solution.py:131
  20.0 53.4 %copy-start.12 = (f32[256,64]{1,0:T(8,128)}, f32[256,64]{1,0:T(8,128)S(1)}, u32[]{:S(2)}) copy-start(f32[256,64]{1,0:T(8,128)S(1)} %get-tuple-element.34) | copy-start | bytes 196612
  259.0 2.8 copy-start.13
  261.8 1.0 copy-start.11
  261.8 1.0 copy-start.15
  265.0 2.8 copy-start.7
  265.0 3.3 copy-start.17
  267.7 0.6 copy-start.21
  273.2 72.2 %all-gather.11.cloned.1.call-start = ((), (), s32[]{:S(2)}) async-start(), calls=%async_computation.4 | async-start | bytes 2621440 | tf_op jit(solution)/shard_map/all_gather | solution.py:130
  279.6 256.3 %all-reduce.4.cloned.1.call-start = ((), (), s32[]{:S(2)}) async-start(), calls=%async_computation.6 | async-start | bytes 16777216 | tf_op jit(solution)/shard_map/psum | solution.py:136
  360.2 185.1 %copy-start.16 = (pred[2,256,256]{1,2,0:T(8,128)(4,1)S(1)}, pred[2,256,256]{1,2,0:T(8,128)(4,1)}, u32[]{:S(2)}) copy-start(pred[2,256,256]{1,2,0:T(8,128)(4,1)} %get-tuple-element.27) | copy-start | bytes 393220
  360.2 185.9 %copy-start.19 = (f32[8192]{0:T(1024)S(1)}, f32[8192]{0:T(1024)}, u32[]{:S(2)}) copy-start(f32[8192]{0:T(1024)} %param.10) | copy-start | bytes 98308
  360.2 185.9 %copy-start.23 = (f32[2,256]{1,0:T(2,128)S(1)}, f32[2,256]{1,0:T(2,128)}, u32[]{:S(2)}) copy-start(f32[2,256]{1,0:T(2,128)} %get-tuple-element.30) | copy-start | bytes 6148
  360.2 220.3 %reduce-scatter.3.cloned.1.call-start = ((), (), s32[]{:S(2)}) async-start(), calls=%async_computation.7 | async-start | bytes 2621440 | tf_op jit(solution)/shard_map/reduce_scatter | solution.py:137
  545.1 139.3 %reduce-scatter.5.cloned.1.call-start = ((), (), s32[]{:S(2)}) async-start(), calls=%async_computation.8 | async-start | bytes 10485760 | tf_op jit(solution)/shard_map/reduce_scatter | solution.py:149
  546.2 37.6 %copy-start.8 = (f32[2,256,256,4]{2,1,3,0:T(8,128)S(1)}, f32[2,256,256,4]{2,1,3,0:T(8,128)}, u32[]{:S(2)}) copy-start(f32[2,256,256,4]{2,1,3,0:T(8,128)} %copy-done.7) | copy-start | bytes 6291460
  583.7 1.7 copy-start.20
  583.7 7.0 slice-start.8
  585.4 4.1 copy-start.14
  585.4 5.3 slice-start.9
  597.8 1.6 copy-start.24
  615.6 2.0 copy-start.2
  745.9 14.9 %copy-start.3 = (f32[512,2048]{1,0:T(8,128)S(1)}, f32[512,2048]{1,0:T(8,128)}, u32[]{:S(2)}) copy-start(f32[512,2048]{1,0:T(8,128)} %copy-done.2) | copy-start | bytes 12582916
  745.9 17.6 %slice-start.4 = ((s8[16777216]{0:T(1024)(128)(4,1)}), s8[4194304]{0:T(1024)(128)(4,1)S(1)}, s32[]{:S(2)}) async-start(s8[16777216]{0:T(1024)(128)(4,1)} %bitcast.142), calls=%async_computation.14 | async-start | bytes 8388608
  745.9 17.6 %slice-start.5 = ((s8[16777216]{0:T(1024)(128)(4,1)}), s8[4194304]{0:T(1024)(128)(4,1)S(1)}, s32[]{:S(2)}) async-start(s8[16777216]{0:T(1024)(128)(4,1)} %bitcast.142), calls=%async_computation.15 | async-start | bytes 8388608
  746.0 17.6 %slice-start.6 = ((s8[16777216]{0:T(1024)(128)(4,1)}), s8[4194304]{0:T(1024)(128)(4,1)S(1)}, s32[]{:S(2)}) async-start(s8[16777216]{0:T(1024)(128)(4,1)} %bitcast.142), calls=%async_computation.16 | async-start | bytes 8388608
  760.8 3.4 slice-start.7
  764.2 7.6 copy-start.10
  764.2 10.6 %slice-start = ((s8[16777216]{0:T(1024)(128)(4,1)}), s8[4194304]{0:T(1024)(128)(4,1)S(1)}, s32[]{:S(2)}) async-start(s8[16777216]{0:T(1024)(128)(4,1)} %bitcast.140), calls=%async_computation.10 | async-start | bytes 8388608
  764.2 10.6 %slice-start.1 = ((s8[16777216]{0:T(1024)(128)(4,1)}), s8[4194304]{0:T(1024)(128)(4,1)S(1)}, s32[]{:S(2)}) async-start(s8[16777216]{0:T(1024)(128)(4,1)} %bitcast.140), calls=%async_computation.11 | async-start | bytes 8388608
  764.2 10.6 %slice-start.2 = ((s8[16777216]{0:T(1024)(128)(4,1)}), s8[4194304]{0:T(1024)(128)(4,1)S(1)}, s32[]{:S(2)}) async-start(s8[16777216]{0:T(1024)(128)(4,1)} %bitcast.140), calls=%async_computation.12 | async-start | bytes 8388608
  771.7 3.5 slice-start.3
  775.2 5.4 copy-start.5
  833.5 12.1 %copy-start.4 = (f32[512,2048]{1,0:T(8,128)S(1)}, f32[512,2048]{1,0:T(8,128)}, u32[]{:S(2)}) copy-start(f32[512,2048]{1,0:T(8,128)} %sub.60) | copy-start | bytes 12582916
  845.5 3.7 copy-start.6
  894.0 4.2 copy-start.9
  894.0 6.6 copy-start.1
Sparse Core Ops, SparseCore 0:
  10.4 55.2 all-gather.6
  68.2 87.4 all-gather.14
  157.5 87.4 all-gather.8
  273.3 35.1 all-gather.12
  310.2 35.1 all-gather.10
  360.3 175.5 all-reduce.3
  545.2 35.2 reduce-scatter.2
  598.0 86.3 reduce-scatter.4
where the time goes:
time: 918 us; the launch traced here: 908 us
  waiting for transfers between devices  508 us (55%)
  other arithmetic  138 us (15%)
  blocking collectives  120 us (13%)
  matrix products  97.7 us (11%)
  local copies, waits for them, and re-layouts  26.5 us (3%)
  between operations  17.1 us (2%)
    psum x1, waiting for transfers between devices, body(): tangent_columns = lax.psum(group_term.astype(jnp.bfloat16), 'tensor')  176 us
    all_gather x1, waiting for transfers between devices, body(): lax.all_gather(dir_query, 'dp', axis=0, tiled=True)  81.5 us
    all_gather x1, waiting for transfers between devices, body(): lax.all_gather(q_weight, 'dp', axis=0, tiled=True)  76.5 us
    reduce_scatter x1, waiting for transfers between devices, body(): lax.psum_scatter((lax.dot_general(normed, cot_query, (((0,), (0,)), ((),...  58.9 us
    psum x1, blocking collectives, body(): lax.psum(local_products(kept_query, kept_output), ('dp', 'tensor'))  40.9 us
    psum x1, blocking collectives, body(): lax.psum(local_products(gn_query, gn_output), ('dp', 'tensor'))  39.5 us
    psum x1, blocking collectives, body(): squares = lax.psum(local_squares, ('dp', 'tensor')) / param_count  39.1 us
    all_gather x1, waiting for transfers between devices, body(): lax.all_gather(kv_pair, 'dp', axis=0, tiled=True)  34.5 us
  transfers between devices with their start and end apart: 8, of which 8 were waited for; matrix products, arithmetic and copies ran while one was open for 10% of the time, Pallas kernels for 0%

commit v1 on v0

--- a/solution.py
+++ b/solution.py
@@ -13,6 +13,35 @@
 ROPE_BASE = 500000.0
 NORM_EPS = 1e-05
 BETA_EPS = 1e-06
+
+
+def values_push(piece_in):
+    mesh_dim = "dp"
+    n_now, ready, response = (lax.axis_size(mesh_dim), lax.axis_index(mesh_dim), piece_in.shape[0])
+    q_next = lax.dynamic_update_slice_in_dim(
+        jnp.zeros(
+            [jj * n_now if b == 0 else jj for b, jj in enumerate(piece_in.shape)], piece_in.dtype
+        ),
+        piece_in,
+        ready * response,
+        axis=0,
+    )
+    o_now = part_now = piece_in
+    for q in range(1, n_now // 2 + 1):
+        o_now = lax.ppermute(
+            o_now, axis_name=mesh_dim, perm=[(b, (b + 1) % n_now) for b in range(n_now)]
+        )
+        q_next = lax.dynamic_update_slice_in_dim(
+            q_next, o_now, (ready - q) % n_now * response, axis=0
+        )
+        if 2 * q < n_now:
+            part_now = lax.ppermute(
+                part_now, axis_name=mesh_dim, perm=[(b, (b - 1) % n_now) for b in range(n_now)]
+            )
+            q_next = lax.dynamic_update_slice_in_dim(
+                q_next, part_now, (ready + q) % n_now * response, axis=0
+            )
+    return q_next
 
 
 def rope_tables(length, head_width):
@@ -95,11 +124,7 @@
     kv_head = lax.axis_index("tensor") * heads_dev // group_size
     kv_columns = lax.dynamic_slice_in_dim(kv_weight, kv_head * HD, HD, 2)
     kv_pair = jnp.concatenate([kv_columns[0], kv_columns[1]], axis=1)
-    sum_query = jnp.dot(
-        normed,
-        lax.all_gather(q_weight, "dp", axis=0, tiled=True),
-        preferred_element_type=jnp.float32,
-    )
+    sum_query = jnp.dot(normed, values_push(q_weight), preferred_element_type=jnp.float32)
     sum_tangent = jnp.dot(
         normed,
         lax.all_gather(dir_query, "dp", axis=0, tiled=True),

time: 918 us -> 940 us (1.024)
  local copies, waits for them, and re-layouts: 26.5 us -> 39.7 us
    ppermute x0 -> x3, waiting for transfers between devices: none -> 196 us  [the longest x2 143 us: values_push(): lax.ppermute(o_now, axis_name=mesh_dim, perm=[(b, (b + 1) % n_now) for b...]
    all_gather x1, waiting for transfers between devices: 81.5 us -> 0.01 us  [body(): lax.all_gather(dir_query, 'dp', axis=0, tiled=True)]
    all_gather x1 -> x0, waiting for transfers between devices: 76.5 us -> none  [body(): lax.all_gather(q_weight, 'dp', axis=0, tiled=True)]
    all_gather x1, waiting for transfers between devices: 34.5 us -> 0.02 us  [body(): lax.all_gather(kv_pair, 'dp', axis=0, tiled=True)]
    dynamic_update_slice x0 -> x4, local copies, waits for them, and re-layouts: none -> 9.48 us  [the longest x2 4.98 us: values_push(): lax.dynamic_update_slice_in_dim(q_next, o_now, (ready - q) % n_now * resp...]
  transfers between devices with their start and end apart: 8 -> 10, of which waited for: 8 -> 8; matrix products, arithmetic and copies ran while one was open for 10% -> 11% of each run, Pallas kernels for 0% -> 0%
where the time goes in v1:
time: 940 us; the launch traced here: 931 us
  waiting for transfers between devices  514 us (55%)
  other arithmetic  139 us (15%)
  blocking collectives  119 us (13%)
  matrix products  94.9 us (10%)
  local copies, waits for them, and re-layouts  39.7 us (4%)
  between operations  17.1 us (2%)
    psum x1, waiting for transfers between devices, body(): tangent_columns = lax.psum(group_term.astype(jnp.bfloat16), 'tensor')  176 us
    ppermute x2, waiting for transfers between devices, values_push(): lax.ppermute(o_now, axis_name=mesh_dim, perm=[(b, (b + 1) % n_now) for b...  143 us
    reduce_scatter x1, waiting for transfers between devices, body(): lax.psum_scatter((lax.dot_general(normed, cot_query, (((0,), (0,)), ((),...  58.9 us
    ppermute x1, waiting for transfers between devices, values_push(): lax.ppermute(part_now, axis_name=mesh_dim, perm=[(b, (b - 1) % n_now) for...  53.4 us
    psum x1, blocking collectives, body(): lax.psum(local_products(kept_query, kept_output), ('dp', 'tensor'))  41 us
    psum x1, blocking collectives, body(): lax.psum(local_products(gn_query, gn_output), ('dp', 'tensor'))  39.5 us
    psum x1, blocking collectives, body(): squares = lax.psum(local_squares, ('dp', 'tensor')) / param_count  39 us
    all_gather x1, waiting for transfers between devices, body(): lax.all_gather(tangent_heads, 'dp', axis=0, tiled=True)  31.4 us
  transfers between devices with their start and end apart: 10, of which 8 were waited for; matrix products, arithmetic and copies ran while one was open for 11% of the time, Pallas kernels for 0%

profile of v1, /device:TPU:0, one launch (start us, length us, event | category | flops | bytes accessed | tf_op | source)
XLA Modules:
  0.0 931.4 jit_solution(16765232784331547087)
XLA Ops:
  7.2 1.4 dynamic-slice_bitcast_fusion.1
  8.7 1.1 pad_maximum_fusion
  9.9 3.0 slice.51
  13.0 3.0 collective-permute-start
  17.0 5.7 multiply_reduce_fusion
  23.3 1.2 fusion.81
  25.5 3.8 broadcast_in_dim.35
  29.3 1.5 constant_dynamic-update-slice_fusion.3
  30.7 65.1 %collective-permute-done = bf16[2048,512]{1,0:T(8,128)(2,1)} collective-permute-done((bf16[2048,512]{1,0:T(8,128)(2,1)}, bf16[2048,512]{1,0:T(8,128)(2,1)}, u32[]{:S(2)}, u32[]{:S(2)}) %collective-permute-start) | collective-permute-done | bytes 2097184 | tf_op jit(solution)/shard_map/ppermute | solution.py:31
  95.9 2.5 collective-permute-start.2
  98.3 10.1 %fusion.9 = bf16[512,8192]{1,0:T(8,128)(2,1)} fusion(f32[8192]{0:T(1024)S(1)} %copy-done.20, f32[512]{0:T(512)S(1)} %bitcast.158, bf16[2,256,8192]{2,1,0:T(8,128)(2,1)} %param.8), kind=kLoop, calls=%fused_computation.18 | loop fusion | flops 16777216 | bytes 16812032 | tf_op jit(solution)/shard_map/convert_element_type | solution.py:95
  108.5 3.5 constant_dynamic-update-slice_fusion.2
  112.0 53.4 %collective-permute-done.1 = bf16[2048,512]{1,0:T(8,128)(2,1)} collective-permute-done((bf16[2048,512]{1,0:T(8,128)(2,1)}, bf16[2048,512]{1,0:T(8,128)(2,1)}, u32[]{:S(2)}, u32[]{:S(2)}) %collective-permute-start.1) | collective-permute-done | bytes 2097184 | tf_op jit(solution)/shard_map/ppermute | solution.py:38
  165.4 3.0 constant_dynamic-update-slice_fusion.1
  168.4 77.9 %collective-permute-done.2 = bf16[2048,512]{1,0:T(8,128)(2,1)S(1)} collective-permute-done((bf16[2048,512]{1,0:T(8,128)(2,1)}, bf16[2048,512]{1,0:T(8,128)(2,1)S(1)}, u32[]{:S(2)}, u32[]{:S(2)}) %collective-permute-start.2) | collective-permute-done | bytes 2097184 | tf_op jit(solution)/shard_map/ppermute | solution.py:31
  246.3 1.5 constant_dynamic-update-slice_fusion
  247.8 8.1 fusion.47
  255.9 1.6 reshape.215
  257.5 6.9 convolution_convert_fusion.2
  266.0 11.2 %fusion.44 = f32[512,512]{1,0:T(8,128)} fusion(bf16[512,8192]{1,0:T(8,128)(2,1)} %fusion.9, bf16[1,8192,512]{2,1,0:T(8,128)(2,1)} %all-gather.12.cloned.1.call-done), kind=kOutput, calls=%fused_computation.59 | convolution fusion | flops 4295753728 | bytes 17825792 | tf_op jit(solution)/shard_map/dot_general | solution.py:128
  277.2 2.5 reshape.217
  279.8 2.8 fusion.92
  283.6 2.2 fusion.28
  285.8 2.7 fusion.30
  289.1 3.0 fusion.48
  292.1 1.3 copy.32
  294.4 3.8 fusion.51
  298.2 1.3 copy.27
  300.4 31.4 %all-gather.10.cloned.1.call-done = bf16[2048,512]{1,0:T(8,128)(2,1)} async-done(((bf16[512,512]{1,0:T(8,128)(2,1)}), bf16[2048,512]{1,0:T(8,128)(2,1)}) %all-gather.10.cloned.1.call-update) | async-done | bytes 2097168 | tf_op jit(solution)/shard_map/all_gather | solution.py:156
  331.8 9.9 %fusion.95 = f32[2048,2048]{1,0:T(8,128)} fusion(bf16[2048,512]{1,0:T(8,128)(2,1)} %all-gather.10.cloned.1.call-done, bf16[512,2048]{1,0:T(8,128)(2,1)S(1)} %copy-done), kind=kOutput, calls=%fused_computation.138 | convolution fusion | flops 4294967296 | bytes 20971520 | tf_op jit(solution)/shard_map/dot_general | solution.py:160
  341.7 27.0 %all-gather.8.cloned.1.call-done = bf16[2048,512]{1,0:T(8,128)(2,1)} async-done(((bf16[512,512]{1,0:T(8,128)(2,1)}), bf16[2048,512]{1,0:T(8,128)(2,1)}) %all-gather.8.cloned.1.call-update) | async-done | bytes 2097168 | tf_op jit(solution)/shard_map/all_gather | solution.py:155
  368.7 14.8 %add_convert_fusion = bf16[2048,2048]{1,0:T(8,128)(2,1)} fusion(f32[2048,2048]{1,0:T(8,128)} %fusion.95, bf16[2048,512]{1,0:T(8,128)(2,1)} %all-gather.8.cloned.1.call-done, bf16[8,512,2048]{2,1,0:T(8,128)(2,1)} %param.15), kind=kOutput, calls=%fused_computation.22 | convolution fusion | flops 4307550208 | bytes 29360128 | tf_op jit(solution)/shard_map/dot_general | solution.py:158
  383.7 175.6 %all-reduce.4.cloned.1.call-done = bf16[2048,2048]{1,0:T(8,128)(2,1)} async-done(((bf16[2048,2048]{1,0:T(8,128)(2,1)}), bf16[2048,2048]{1,0:T(8,128)(2,1)}) %all-reduce.4.cloned.1.call-update) | async-done | bytes 8388624 | tf_op jit(solution)/shard_map/psum | solution.py:161
  559.3 9.3 convolution_convert_fusion
  569.5 10.0 %multiply_convert_fusion.2 = bf16[2,256,8192]{2,1,0:T(8,128)(2,1)} fusion(f32[8192]{0:T(1024)S(1)} %copy-done.21, f32[2,256]{1,0:T(2,128)S(1)} %copy-done.25, bf16[2,256,8192]{2,1,0:T(8,128)(2,1)} %param.8), kind=kLoop, calls=%fused_computation.23 | loop fusion | flops 16777216 | bytes 16812032 | tf_op jit(solution)/shard_map/convert_element_type | solution.py:95
  579.5 24.5 %reduce-scatter.3.cloned.1.call-done = bf16[512,512]{1,0:T(8,128)(2,1)} async-done(((bf16[2048,512]{1,0:T(8,128)(2,1)}), bf16[512,512]{1,0:T(8,128)(2,1)}) %reduce-scatter.3.cloned.1.call-update) | async-done | bytes 524304 | tf_op jit(solution)/shard_map/reduce_scatter | solution.py:162
  604.0 2.0 reshape.208
  606.0 1.3 copy.33
  607.3 1.6 multiply_reduce_fusion.3
  609.0 4.0 fusion.26
  614.3 7.1 multiply_convert_fusion.1
  621.4 1.6 copy-done.26
  623.0 10.2 %multiply_convert_fusion = bf16[4,512,2048]{2,1,0:T(8,128)(2,1)} fusion(bf16[4,512,512]{2,1,0:T(8,128)(2,1)S(1)} %bitcast.160, bf16[4,512,2048]{2,1,0:T(8,128)(2,1)} %bitcast.159), kind=kOutput, calls=%fused_computation.20 | convolution fusion | flops 4303355904 | bytes 18874368 | tf_op jit(solution)/shard_map/nta,ntb->nab/dot_general | solution.py:102
  633.2 5.9 convert_reduce_fusion
  639.2 2.0 copy-done.2
  641.1 7.8 fusion.4
  649.0 58.9 %reduce-scatter.5.cloned.1.call-done = bf16[2048,512]{1,0:T(8,128)(2,1)} async-done(((bf16[8192,512]{1,0:T(8,128)(2,1)}), bf16[2048,512]{1,0:T(8,128)(2,1)}) %reduce-scatter.5.cloned.1.call-update) | async-done | bytes 2097168 | tf_op jit(solution)/shard_map/reduce_scatter | solution.py:174
  707.9 2.2 convert_element_type.110
  710.1 8.0 fusion
  718.0 39.5 %psum.29 = f32[8]{0:T(128)S(1)} all-reduce(f32[8]{0:T(128)S(1)} %add.104), channel_id=1, replica_groups=mesh['dp'=4,'tensor'=8] {'dp','tensor'}, use_global_device_ids=true, to_apply=%region_11.12 | all-reduce | flops 8 | bytes 64 | tf_op jit(solution)/shard_map/psum | solution.py:199
  757.5 11.9 %fusion.5 = f32[512,2048]{1,0:T(8,128)S(1)} fusion(bf16[8,512,2048]{2,1,0:T(8,128)(2,1)} %param.15, f32[8]{0:T(128)S(1)} %broadcast_multiply_fusion.1), kind=kLoop, calls=%fused_computation.13 | loop fusion | flops 24117248 | bytes 20971552 | tf_op jit(solution)/shard_map/reduce_sum | solution.py:196
  769.5 14.8 %fusion.1 = f32[2048,512]{1,0:T(8,128)} fusion(bf16[8,2048,512]{2,1,0:T(8,128)(2,1)} %param.14, f32[8]{0:T(128)S(1)} %broadcast_multiply_fusion.1), kind=kLoop, calls=%fused_computation.9 | loop fusion | flops 24117248 | bytes 20971552 | tf_op jit(solution)/shard_map/reduce_sum | solution.py:194
  784.3 2.8 sub.68
  787.7 7.6 fusion.6
  795.3 3.1 convert_subtract_fusion
  798.7 5.4 fusion.2
  804.1 41.0 %psum.30 = f32[8]{0:T(128)S(1)} all-reduce(f32[8]{0:T(128)S(1)} %add.105), channel_id=1, replica_groups=mesh['dp'=4,'tensor'=8] {'dp','tensor'}, use_global_device_ids=true, to_apply=%region_16.17 | all-reduce | flops 8 | bytes 64 | tf_op jit(solution)/shard_map/psum | solution.py:202
  845.1 11.9 %fusion.7 = f32[512,2048]{1,0:T(8,128)S(1)} fusion(bf16[8,512,2048]{2,1,0:T(8,128)(2,1)} %param.15, f32[8]{0:T(128)S(1)} %get-tuple-element.32), kind=kLoop, calls=%fused_computation.15 | loop fusion | flops 24117248 | bytes 20971552 | tf_op jit(solution)/shard_map/reduce_sum | solution.py:196
  857.0 12.1 %fusion.3 = f32[2048,512]{1,0:T(8,128)S(1)} fusion(bf16[8,2048,512]{2,1,0:T(8,128)(2,1)} %param.14, f32[8]{0:T(128)S(1)} %get-tuple-element.32), kind=kLoop, calls=%fused_computation.11 | loop fusion | flops 24117248 | bytes 20971552 | tf_op jit(solution)/shard_map/reduce_sum | solution.py:194
  869.1 3.6 multiply_reduce_fusion.1
  872.8 3.7 multiply_reduce_fusion.2
  877.7 39.0 %psum.31 = f32[]{:T(128)} all-reduce(f32[]{:T(128)S(6)} %add.106), channel_id=1, replica_groups=mesh['dp'=4,'tensor'=8] {'dp','tensor'}, use_global_device_ids=true, to_apply=%region_21.22 | all-reduce | flops 1 | bytes 8 | tf_op jit(solution)/shard_map/psum | solution.py:206
  917.5 4.1 divide_convert_fusion
  921.7 1.9 divide_convert_fusion.1
  (115 shorter events, 11.7 us)
Async XLA Ops:
  7.2 324.7 %copy-start = (bf16[512,2048]{1,0:T(8,128)(2,1)S(1)}, bf16[512,2048]{1,0:T(8,128)(2,1)}, u32[]{:S(2)}) copy-start(bf16[512,2048]{1,0:T(8,128)(2,1)} %param.13) | copy-start | bytes 6291460
  7.2 250.3 %all-gather.6.cloned.1.call-start = ((), (), s32[]{:S(2)}) async-start(), calls=%async_computation.2 | async-start | bytes 5242880 | tf_op jit(solution)/shard_map/all_gather | solution.py:135
  9.8 256.2 %all-gather.12.cloned.1.call-start = ((), (), s32[]{:S(2)}) async-start(), calls=%async_computation.8 | async-start | bytes 10485760 | tf_op jit(solution)/shard_map/all_gather | solution.py:130
  12.9 318.9 %all-gather.10.cloned.1.call-start = ((), (), s32[]{:S(2)}) async-start(), calls=%async_computation.4 | async-start | bytes 2621440 | tf_op jit(solution)/shard_map/all_gather | solution.py:156
  13.0 82.9 %collective-permute-start = (bf16[2048,512]{1,0:T(8,128)(2,1)}, bf16[2048,512]{1,0:T(8,128)(2,1)}, u32[]{:S(2)}, u32[]{:S(2)}) collective-permute-start(bf16[2048,512]{1,0:T(8,128)(2,1)} %param.11), channel_id=1, source_target_pairs={{0,8},{8,16},{16,24},{24,0},{1,9},{9,17},{17,25},{25,1},{2,10},{10... | collective-permute-start | bytes 6291464 | tf_op jit(solution)/shard_map/ppermute | solution.py:31
  16.0 149.4 %collective-permute-start.1 = (bf16[2048,512]{1,0:T(8,128)(2,1)}, bf16[2048,512]{1,0:T(8,128)(2,1)}, u32[]{:S(2)}, u32[]{:S(2)}) collective-permute-start(bf16[2048,512]{1,0:T(8,128)(2,1)} %param.11), channel_id=1, source_target_pairs={{0,24},{8,0},{16,8},{24,16},{1,25},{9,1},{17,9},{25,17},{2,26},{10... | collective-permute-start | bytes 6291464 | tf_op jit(solution)/shard_map/ppermute | solution.py:38
  17.0 7.5 copy-start.24
  25.5 3.8 copy-start.17
  29.3 69.1 %copy-start.20 = (f32[8192]{0:T(1024)S(1)}, f32[8192]{0:T(1024)}, u32[]{:S(2)}) copy-start(f32[8192]{0:T(1024)} %param.10) | copy-start | bytes 98308
  95.9 150.5 %collective-permute-start.2 = (bf16[2048,512]{1,0:T(8,128)(2,1)}, bf16[2048,512]{1,0:T(8,128)(2,1)S(1)}, u32[]{:S(2)}, u32[]{:S(2)}) collective-permute-start(bf16[2048,512]{1,0:T(8,128)(2,1)} %collective-permute-done), channel_id=1, source_target_pairs={{0,8},{8,16},{16,24},{24,0},{1,9},{9,17},{17,25},{25,1},{2,10},{10... | collective-permute-start | bytes 6291464 | tf_op jit(solution)/shard_map/ppermute | solution.py:31
  112.0 135.9 %copy-start.11 = (bf16[512,8192]{1,0:T(8,128)(2,1)S(1)}, bf16[512,8192]{1,0:T(8,128)(2,1)}, u32[]{:S(2)}) copy-start(bf16[512,8192]{1,0:T(8,128)(2,1)} %fusion.9) | copy-start | bytes 25165828
  257.5 7.6 copy-start.13
  279.8 2.8 copy-start.14
  282.6 1.0 copy-start.12
  282.6 1.0 copy-start.16
  285.8 2.8 copy-start.7
  285.8 3.3 copy-start.19
  288.5 0.6 copy-start.23
  294.3 74.4 %all-gather.8.cloned.1.call-start = ((), (), s32[]{:S(2)}) async-start(), calls=%async_computation.3 | async-start | bytes 2621440 | tf_op jit(solution)/shard_map/all_gather | solution.py:155
  300.4 258.9 %all-reduce.4.cloned.1.call-start = ((), (), s32[]{:S(2)}) async-start(), calls=%async_computation.5 | async-start | bytes 16777216 | tf_op jit(solution)/shard_map/psum | solution.py:161
  383.6 185.1 %copy-start.18 = (pred[2,256,256]{1,2,0:T(8,128)(4,1)S(1)}, pred[2,256,256]{1,2,0:T(8,128)(4,1)}, u32[]{:S(2)}) copy-start(pred[2,256,256]{1,2,0:T(8,128)(4,1)} %get-tuple-element.27) | copy-start | bytes 393220
  383.6 185.9 %copy-start.21 = (f32[8192]{0:T(1024)S(1)}, f32[8192]{0:T(1024)}, u32[]{:S(2)}) copy-start(f32[8192]{0:T(1024)} %param.10) | copy-start | bytes 98308
  383.6 185.9 %copy-start.25 = (f32[2,256]{1,0:T(2,128)S(1)}, f32[2,256]{1,0:T(2,128)}, u32[]{:S(2)}) copy-start(f32[2,256]{1,0:T(2,128)} %get-tuple-element.30) | copy-start | bytes 6148
  383.6 220.4 %reduce-scatter.3.cloned.1.call-start = ((), (), s32[]{:S(2)}) async-start(), calls=%async_computation.6 | async-start | bytes 2621440 | tf_op jit(solution)/shard_map/reduce_scatter | solution.py:162
  568.6 139.3 %reduce-scatter.5.cloned.1.call-start = ((), (), s32[]{:S(2)}) async-start(), calls=%async_computation.7 | async-start | bytes 10485760 | tf_op jit(solution)/shard_map/reduce_scatter | solution.py:174
  569.5 37.8 %copy-start.8 = (f32[2,256,256,4]{2,1,3,0:T(8,128)S(1)}, f32[2,256,256,4]{2,1,3,0:T(8,128)}, u32[]{:S(2)}) copy-start(f32[2,256,256,4]{2,1,3,0:T(8,128)} %copy-done.7) | copy-start | bytes 6291460
  607.3 1.7 copy-start.22
  607.3 7.0 slice-start.8
  609.0 4.1 copy-start.15
  609.0 5.3 slice-start.9
  621.4 1.6 copy-start.26
  639.2 2.0 copy-start.2
  769.5 14.8 %copy-start.3 = (f32[512,2048]{1,0:T(8,128)S(1)}, f32[512,2048]{1,0:T(8,128)}, u32[]{:S(2)}) copy-start(f32[512,2048]{1,0:T(8,128)} %copy-done.2) | copy-start | bytes 12582916
  769.5 17.6 %slice-start.4 = ((s8[16777216]{0:T(1024)(128)(4,1)}), s8[4194304]{0:T(1024)(128)(4,1)S(1)}, s32[]{:S(2)}) async-start(s8[16777216]{0:T(1024)(128)(4,1)} %bitcast.142), calls=%async_computation.13 | async-start | bytes 8388608
  769.5 17.6 %slice-start.5 = ((s8[16777216]{0:T(1024)(128)(4,1)}), s8[4194304]{0:T(1024)(128)(4,1)S(1)}, s32[]{:S(2)}) async-start(s8[16777216]{0:T(1024)(128)(4,1)} %bitcast.142), calls=%async_computation.14 | async-start | bytes 8388608
  769.5 17.6 %slice-start.6 = ((s8[16777216]{0:T(1024)(128)(4,1)}), s8[4194304]{0:T(1024)(128)(4,1)S(1)}, s32[]{:S(2)}) async-start(s8[16777216]{0:T(1024)(128)(4,1)} %bitcast.142), calls=%async_computation.15 | async-start | bytes 8388608
  784.3 3.4 slice-start.7
  787.7 7.6 copy-start.10
  787.7 10.6 %slice-start = ((s8[16777216]{0:T(1024)(128)(4,1)}), s8[4194304]{0:T(1024)(128)(4,1)S(1)}, s32[]{:S(2)}) async-start(s8[16777216]{0:T(1024)(128)(4,1)} %bitcast.140), calls=%async_computation.9 | async-start | bytes 8388608
  787.7 10.6 %slice-start.1 = ((s8[16777216]{0:T(1024)(128)(4,1)}), s8[4194304]{0:T(1024)(128)(4,1)S(1)}, s32[]{:S(2)}) async-start(s8[16777216]{0:T(1024)(128)(4,1)} %bitcast.140), calls=%async_computation.10 | async-start | bytes 8388608
  787.7 10.6 %slice-start.2 = ((s8[16777216]{0:T(1024)(128)(4,1)}), s8[4194304]{0:T(1024)(128)(4,1)S(1)}, s32[]{:S(2)}) async-start(s8[16777216]{0:T(1024)(128)(4,1)} %bitcast.140), calls=%async_computation.11 | async-start | bytes 8388608
  795.3 3.5 slice-start.3
  798.7 5.4 copy-start.5
  857.0 12.1 %copy-start.4 = (f32[512,2048]{1,0:T(8,128)S(1)}, f32[512,2048]{1,0:T(8,128)}, u32[]{:S(2)}) copy-start(f32[512,2048]{1,0:T(8,128)} %sub.68) | copy-start | bytes 12582916
  869.1 3.7 copy-start.6
  917.5 4.2 copy-start.9
  917.5 6.6 copy-start.1
Sparse Core Ops, SparseCore 0:
  9.9 88.6 all-gather.5
  101.1 153.2 all-gather.11
  294.5 37.3 all-gather.9
  333.5 35.1 all-gather.7
  383.7 175.5 all-reduce.3
  568.7 35.2 reduce-scatter.2
  621.5 86.3 reduce-scatter.4
